TPU v7x, 32 devices: a whole 2x2x4 slice. The times are simulated.
32 devices in a mesh: lists: 4 (over y, x), points: 8 (over z, core).
Axes of the slice: x: 2, y: 2, z: 4, core: 2. Of those that a mesh axis runs over, the one named last changes fastest.
Arguments:
- child_centroids: float32 [1024, 768], P(('lists', 'points')), may hold values from -6 to 6
- child_sizes: int32 [1024], P(('lists', 'points')), may hold values from 1 to 256
- parent_of: int32 [1024], P(('lists', 'points')), may hold values from 0 to 511, as said below
- points: bfloat16 [49152, 768], P(('lists', 'points')), may hold values from -6 to 6
- assign: int32 [49152], P(('lists', 'points')), may hold values from 0 to 127
- codes: int32 [49152, 96], P(('lists', 'points')), may hold values from 0 to 255
- rotation: bfloat16 [768, 768], replicated, may hold values from -0.21875 to 0.21875
Outputs:
- merged_centroids: float32 [512, 768], P(('lists', 'points'))
- codeword_means: float32 [768, 256], replicated
Inputs may be any that keep to these rules, and one draw needn't show every extreme that they name: `parent_of`: every parent has exactly two children. Of the 32 children of one device, at most 16 have parents in one block of 128 consecutive parent numbers, and exactly 16 in some block.
All inputs are finite; a program needn't handle non-finite values.
Results may differ from a plain program's by a relative error of at most 0.0042.
Values may be sent and summed in bfloat16 or wider, within the bound.
No kernel may reach another device: no remote copies, remote signals or barrier semaphores. Data moves between devices by JAX's collectives and lax.ppermute only.
A program may use at most 64 MiB of HBM per device.

v0:
```python
import jax
import jax.numpy as jnp
from jax import lax
from jax.sharding import PartitionSpec as P

CODEWORDS = 256


def body(child_centroids, child_sizes, parent_of, points, assign, codes, rotation):
    columns = lax.axis_size("points")
    child_count = child_centroids.shape[0]
    feature_width = child_centroids.shape[1]
    owner_parents = columns * child_count // 2
    child_weight = child_sizes.astype(jnp.float32)
    weighted = child_weight[:, None] * child_centroids
    all_rows, all_mass, all_parent = (
        lax.all_gather(weighted, "lists", axis=0, tiled=True),
        lax.all_gather(child_weight, "lists", axis=0, tiled=True),
        lax.all_gather(parent_of.astype(jnp.float32), "lists", axis=0, tiled=True),
    )
    parent_whole = all_parent.astype(jnp.int32)
    first_parent = lax.axis_index("lists") * owner_parents
    owned_here = (parent_whole >= first_parent) & (parent_whole < first_parent + owner_parents)
    got_rows = jnp.where(owned_here[:, None], all_rows, 0.0)
    got_mass = jnp.where(owned_here, all_mass, 0.0)
    seg_target = jnp.where(owned_here, parent_whole - first_parent, 0)
    partial_sum = jax.ops.segment_sum(got_rows, seg_target, num_segments=owner_parents)
    partial_mass = jax.ops.segment_sum(got_mass, seg_target, num_segments=owner_parents)
    shard_rows = owner_parents // columns
    total_sum, total_mass = lax.psum((partial_sum, partial_mass), "points")
    merged_all = total_sum / total_mass[:, None]
    lowered = merged_all.astype(jnp.bfloat16)
    merged = lax.dynamic_slice_in_dim(
        merged_all, lax.axis_index("points") * shard_rows, shard_rows, 0
    )
    chosen = jnp.take(lowered, assign, axis=0)
    residual = (points.astype(jnp.float32) - chosen.astype(jnp.float32)).astype(jnp.bfloat16)
    rotated = jnp.dot(residual, rotation, preferred_element_type=jnp.float32).astype(jnp.bfloat16)
    point_count = points.shape[0]
    subspaces = codes.shape[1]
    sub_width = feature_width // subspaces
    block_rows = min(128, point_count)
    block_count = point_count // block_rows
    codeword_ids = jnp.arange(CODEWORDS, dtype=jnp.int32)

    def accumulate(carried, block_inputs):
        code_sums, code_counts = carried
        rot_blk, code_blk = block_inputs
        onehot = (code_blk[:, :, None] == codeword_ids[None, None, :]).astype(jnp.bfloat16)
        code_sums = code_sums + jnp.einsum(
            "pmd,pmk->mdk", rot_blk, onehot, preferred_element_type=jnp.float32
        )
        code_counts = code_counts + jnp.sum(onehot, axis=0, dtype=jnp.float32)
        return ((code_sums, code_counts), None)

    initial = (
        jnp.zeros((subspaces, sub_width, CODEWORDS), jnp.float32),
        jnp.zeros((subspaces, CODEWORDS), jnp.float32),
    )
    (code_sums, code_counts), _ = lax.scan(
        accumulate,
        initial,
        (
            rotated.reshape(block_count, block_rows, subspaces, sub_width),
            codes.reshape(block_count, block_rows, subspaces),
        ),
    )
    total_sums, total_counts = lax.psum(
        (code_sums.reshape(feature_width, CODEWORDS), code_counts), ("lists", "points")
    )
    means = total_sums.reshape(subspaces, sub_width, CODEWORDS) / (1.0 + total_counts[:, None, :])
    return (merged, means.reshape(feature_width, CODEWORDS))


def solution(mesh):
    in_specs = (
        P(("lists", "points"), None),
        P(("lists", "points")),
        P(("lists", "points")),
        P(("lists", "points"), None),
        P(("lists", "points")),
        P(("lists", "points"), None),
        P(),
    )
    out_specs = (P(("lists", "points"), None), P())
    return jax.shard_map(body, mesh=mesh, in_specs=in_specs, out_specs=out_specs, check_vma=False)
```

profile of v0, /device:TPU:0, one launch (start us, length us, event | category | flops | bytes accessed | tf_op | source)
XLA Modules:
  0.0 357.0 jit_solution(9061663071165604065)
XLA Ops:
  11.5 11.3 %all-reduce.3 = (f32[128]{0:T(128)S(1)}, f32[128]{0:T(128)S(1)}) all-reduce(f32[128]{0:T(128)S(1)} %convert_dynamic-update-slice_fusion, f32[128]{0:T(128)S(1)} %convert_dynamic-update-slice_fusion.1), channel_id=1, replica_groups=mesh['lists'=4,'points'=8] {'lists'}, use_global_device_ids=true, to_apply=%add | all-reduce | flops 256 | bytes 2048
  23.8 9.0 %all_gather.10 = f32[128,768]{1,0:T(8,128)S(1)} all-gather(f32[32,768]{1,0:T(8,128)S(1)} %broadcast_multiply_fusion), channel_id=1, replica_groups=mesh['lists'=4,'points'=8] {'lists'}, dimensions={0}, use_global_device_ids=true | all-gather | bytes 491520 | tf_op jit(solution)/shard_map/all_gather | solution.py:17
  36.5 13.8 %psum.29 = f32[128]{0:T(128)S(1)} all-reduce(f32[128]{0:T(128)S(1)} %scatter_custom_fusion.1), channel_id=1, replica_groups=mesh['lists'=4,'points'=8] {'points'}, use_global_device_ids=true, to_apply=%region_3.4 | all-reduce | flops 128 | bytes 1024 | tf_op jit(solution)/shard_map/psum | solution.py:30
  52.1 39.0 %all-reduce.7.cloned.1.call-done = f32[128,768]{1,0:T(8,128)} async-done(((f32[128,768]{1,0:T(8,128)}), f32[128,768]{1,0:T(8,128)}) %all-reduce.7.cloned.1.call-update) | async-done | bytes 393232 | tf_op jit(solution)/shard_map/psum | solution.py:30
  92.9 5.7 %gather_fusion = bf16[1536,768]{1,0:T(8,128)(2,1)} fusion(bf16[128,768]{1,0:T(8,128)(2,1)S(1)} %get-tuple-element.81, s32[2048]{0:T(1024)S(1)} %pad_clamp_fusion), kind=kCustom, calls=%fused_computation | custom fusion | bytes 4724736 | tf_op jit(solution)/shard_map/jit(_take)/gather | solution.py:36
  98.6 6.0 %convolution_convert_fusion = bf16[1536,768]{1,0:T(8,128)(2,1)} fusion(bf16[768,768]{1,0:T(8,128)(2,1)S(1)} %copy-done, bf16[1536,768]{1,0:T(8,128)(2,1)} %param.12, bf16[1536,768]{1,0:T(8,128)(2,1)} %gather_fusion, pred[1536]{0:T(1024)(128)(4,1)S(1)} %compare_and_fusion), kind=kOutput, calls=%fused_computation.16 | convolution fusion | flops 1819017216 | bytes 8259072 | tf_op jit(solution)/shard_map/dot_general | solution.py:38
  104.6 2.8 copy.10
  107.4 3.1 reshape.29
  110.5 4.0 %copy.11 = bf16[12,128,96,8]{1,3,2,0:T(8,128)(2,1)} copy(bf16[12,128,96,8]{1,0,3,2:T(8,128)(2,1)} %reshape.29) | data formatting | bytes 4718592
  114.5 103.4 %while.13 = (s32[]{:T(128)}, f32[96,8,256]{2,1,0:T(8,128)S(1)}, f32[96,256]{1,0:T(8,128)S(1)}, bf16[12,128,96,8]{1,3,2,0:T(8,128)(2,1)}, s32[12,128,96]{1,0,2:T(8,128)}, /*index=5*/s32[]{:T(128)}, s32[]{:T(128)}) while((s32[]{:T(128)}, f32[96,8,256]{2,1,0:T(8,128)S(1)}, f32[96,256]{1,0:T(8,128)S(1)}, ...), condition=%wide.region_6.7_spmd.clone, body=%wide.region_4.6_spmd.clone.sunk | while | flops 66478080 | bytes 2359900 | solution.py:60
  115.6 5.1 %fusion.23 = f32[96,8,256]{2,1,0:T(8,128)S(1)} fusion(s32[128,96]{0,1:T(8,128)S(1)} %bitcast.19, f32[96,8,256]{2,1,0:T(8,128)S(1)} %get-tuple-element.124, pred[]{:T(512)S(6)} %compare.3, bf16[12,128,96,8]{1,3,2,0:T(8,128)(2,1)} %get-tuple-element.133, s32[]{:T(128)} %get-tuple-element.123), kind=kOutput, calls=%fused_computation.9.clone.1 | convolution fusion | flops 53870592 | bytes 1819137 | tf_op jit(solution)/shard_map/while/body/eval_jaxpr/pmd,pmk->mdk/dot_general | solution.py:50
  120.6 2.5 convert_reduce_fusion.2
  124.2 5.1 %fusion.23 = f32[96,8,256]{2,1,0:T(8,128)S(1)} fusion(s32[128,96]{0,1:T(8,128)S(1)} %bitcast.19, f32[96,8,256]{2,1,0:T(8,128)S(1)} %get-tuple-element.124, pred[]{:T(512)S(6)} %compare.3, bf16[12,128,96,8]{1,3,2,0:T(8,128)(2,1)} %get-tuple-element.133, s32[]{:T(128)} %get-tuple-element.123), kind=kOutput, calls=%fused_computation.9.clone.1 | convolution fusion | flops 53870592 | bytes 1819137 | tf_op jit(solution)/shard_map/while/body/eval_jaxpr/pmd,pmk->mdk/dot_general | solution.py:50
  129.2 2.5 convert_reduce_fusion.2
  132.8 5.1 %fusion.23 = f32[96,8,256]{2,1,0:T(8,128)S(1)} fusion(s32[128,96]{0,1:T(8,128)S(1)} %bitcast.19, f32[96,8,256]{2,1,0:T(8,128)S(1)} %get-tuple-element.124, pred[]{:T(512)S(6)} %compare.3, bf16[12,128,96,8]{1,3,2,0:T(8,128)(2,1)} %get-tuple-element.133, s32[]{:T(128)} %get-tuple-element.123), kind=kOutput, calls=%fused_computation.9.clone.1 | convolution fusion | flops 53870592 | bytes 1819137 | tf_op jit(solution)/shard_map/while/body/eval_jaxpr/pmd,pmk->mdk/dot_general | solution.py:50
  137.9 2.5 convert_reduce_fusion.2
  141.4 5.1 %fusion.23 = f32[96,8,256]{2,1,0:T(8,128)S(1)} fusion(s32[128,96]{0,1:T(8,128)S(1)} %bitcast.19, f32[96,8,256]{2,1,0:T(8,128)S(1)} %get-tuple-element.124, pred[]{:T(512)S(6)} %compare.3, bf16[12,128,96,8]{1,3,2,0:T(8,128)(2,1)} %get-tuple-element.133, s32[]{:T(128)} %get-tuple-element.123), kind=kOutput, calls=%fused_computation.9.clone.1 | convolution fusion | flops 53870592 | bytes 1819137 | tf_op jit(solution)/shard_map/while/body/eval_jaxpr/pmd,pmk->mdk/dot_general | solution.py:50
  146.5 2.5 convert_reduce_fusion.2
  150.0 5.1 %fusion.23 = f32[96,8,256]{2,1,0:T(8,128)S(1)} fusion(s32[128,96]{0,1:T(8,128)S(1)} %bitcast.19, f32[96,8,256]{2,1,0:T(8,128)S(1)} %get-tuple-element.124, pred[]{:T(512)S(6)} %compare.3, bf16[12,128,96,8]{1,3,2,0:T(8,128)(2,1)} %get-tuple-element.133, s32[]{:T(128)} %get-tuple-element.123), kind=kOutput, calls=%fused_computation.9.clone.1 | convolution fusion | flops 53870592 | bytes 1819137 | tf_op jit(solution)/shard_map/while/body/eval_jaxpr/pmd,pmk->mdk/dot_general | solution.py:50
  155.1 2.5 convert_reduce_fusion.2
  158.7 5.1 %fusion.23 = f32[96,8,256]{2,1,0:T(8,128)S(1)} fusion(s32[128,96]{0,1:T(8,128)S(1)} %bitcast.19, f32[96,8,256]{2,1,0:T(8,128)S(1)} %get-tuple-element.124, pred[]{:T(512)S(6)} %compare.3, bf16[12,128,96,8]{1,3,2,0:T(8,128)(2,1)} %get-tuple-element.133, s32[]{:T(128)} %get-tuple-element.123), kind=kOutput, calls=%fused_computation.9.clone.1 | convolution fusion | flops 53870592 | bytes 1819137 | tf_op jit(solution)/shard_map/while/body/eval_jaxpr/pmd,pmk->mdk/dot_general | solution.py:50
  163.7 2.5 convert_reduce_fusion.2
  167.3 5.1 %fusion.23 = f32[96,8,256]{2,1,0:T(8,128)S(1)} fusion(s32[128,96]{0,1:T(8,128)S(1)} %bitcast.19, f32[96,8,256]{2,1,0:T(8,128)S(1)} %get-tuple-element.124, pred[]{:T(512)S(6)} %compare.3, bf16[12,128,96,8]{1,3,2,0:T(8,128)(2,1)} %get-tuple-element.133, s32[]{:T(128)} %get-tuple-element.123), kind=kOutput, calls=%fused_computation.9.clone.1 | convolution fusion | flops 53870592 | bytes 1819137 | tf_op jit(solution)/shard_map/while/body/eval_jaxpr/pmd,pmk->mdk/dot_general | solution.py:50
  175.9 5.1 %fusion.23 = f32[96,8,256]{2,1,0:T(8,128)S(1)} fusion(s32[128,96]{0,1:T(8,128)S(1)} %bitcast.19, f32[96,8,256]{2,1,0:T(8,128)S(1)} %get-tuple-element.124, pred[]{:T(512)S(6)} %compare.3, bf16[12,128,96,8]{1,3,2,0:T(8,128)(2,1)} %get-tuple-element.133, s32[]{:T(128)} %get-tuple-element.123), kind=kOutput, calls=%fused_computation.9.clone.1 | convolution fusion | flops 53870592 | bytes 1819137 | tf_op jit(solution)/shard_map/while/body/eval_jaxpr/pmd,pmk->mdk/dot_general | solution.py:50
  181.0 2.5 convert_reduce_fusion.2
  184.5 5.1 %fusion.23 = f32[96,8,256]{2,1,0:T(8,128)S(1)} fusion(s32[128,96]{0,1:T(8,128)S(1)} %bitcast.19, f32[96,8,256]{2,1,0:T(8,128)S(1)} %get-tuple-element.124, pred[]{:T(512)S(6)} %compare.3, bf16[12,128,96,8]{1,3,2,0:T(8,128)(2,1)} %get-tuple-element.133, s32[]{:T(128)} %get-tuple-element.123), kind=kOutput, calls=%fused_computation.9.clone.1 | convolution fusion | flops 53870592 | bytes 1819137 | tf_op jit(solution)/shard_map/while/body/eval_jaxpr/pmd,pmk->mdk/dot_general | solution.py:50
  189.6 2.5 convert_reduce_fusion.2
  193.1 5.1 %fusion.23 = f32[96,8,256]{2,1,0:T(8,128)S(1)} fusion(s32[128,96]{0,1:T(8,128)S(1)} %bitcast.19, f32[96,8,256]{2,1,0:T(8,128)S(1)} %get-tuple-element.124, pred[]{:T(512)S(6)} %compare.3, bf16[12,128,96,8]{1,3,2,0:T(8,128)(2,1)} %get-tuple-element.133, s32[]{:T(128)} %get-tuple-element.123), kind=kOutput, calls=%fused_computation.9.clone.1 | convolution fusion | flops 53870592 | bytes 1819137 | tf_op jit(solution)/shard_map/while/body/eval_jaxpr/pmd,pmk->mdk/dot_general | solution.py:50
  201.8 5.1 %fusion.23 = f32[96,8,256]{2,1,0:T(8,128)S(1)} fusion(s32[128,96]{0,1:T(8,128)S(1)} %bitcast.19, f32[96,8,256]{2,1,0:T(8,128)S(1)} %get-tuple-element.124, pred[]{:T(512)S(6)} %compare.3, bf16[12,128,96,8]{1,3,2,0:T(8,128)(2,1)} %get-tuple-element.133, s32[]{:T(128)} %get-tuple-element.123), kind=kOutput, calls=%fused_computation.9.clone.1 | convolution fusion | flops 53870592 | bytes 1819137 | tf_op jit(solution)/shard_map/while/body/eval_jaxpr/pmd,pmk->mdk/dot_general | solution.py:50
  210.4 5.1 %fusion.23 = f32[96,8,256]{2,1,0:T(8,128)S(1)} fusion(s32[128,96]{0,1:T(8,128)S(1)} %bitcast.19, f32[96,8,256]{2,1,0:T(8,128)S(1)} %get-tuple-element.124, pred[]{:T(512)S(6)} %compare.3, bf16[12,128,96,8]{1,3,2,0:T(8,128)(2,1)} %get-tuple-element.133, s32[]{:T(128)} %get-tuple-element.123), kind=kOutput, calls=%fused_computation.9.clone.1 | convolution fusion | flops 53870592 | bytes 1819137 | tf_op jit(solution)/shard_map/while/body/eval_jaxpr/pmd,pmk->mdk/dot_general | solution.py:50
  215.4 2.5 convert_reduce_fusion.2
  220.3 126.8 %all-reduce.9.cloned.1.call-done = (f32[768,256]{1,0:T(8,128)}, f32[96,256]{1,0:T(8,128)}) async-done(((f32[768,256]{1,0:T(8,128)}, f32[96,256]{1,0:T(8,128)}), (f32[768,256]{1,0:T(8,128)}, f32[96,256]{1,0:T(8,128)})) %all-reduce.9.cloned.1.call-update) | async-done | bytes 884752 | tf_op jit(solution)/shard_map/psum | solution.py:68
  (66 shorter events, 37.5 us)
Async XLA Ops:
  7.2 91.4 %copy-start = (bf16[768,768]{1,0:T(8,128)(2,1)S(1)}, bf16[768,768]{1,0:T(8,128)(2,1)}, u32[]{:S(2)}) copy-start(bf16[768,768]{1,0:T(8,128)(2,1)} %param.15) | copy-start | bytes 3538948
  7.2 44.9 %copy-start.6 = (s32[1536]{0:T(1024)S(1)}, s32[1536]{0:T(1024)}, u32[]{:S(2)}) copy-start(s32[1536]{0:T(1024)} %param.13) | copy-start | bytes 18436
  7.2 43.8 %copy-start.5 = (s32[1536,96]{0,1:T(8,128)S(1)}, s32[1536,96]{0,1:T(8,128)}, u32[]{:S(2)}) copy-start(s32[1536,96]{0,1:T(8,128)} %param.14) | copy-start | bytes 1769476
  7.2 83.8 %all-reduce.7.cloned.1.call-start = ((), (), s32[]{:S(2)}) async-start(), calls=%async_computation | async-start | bytes 786432 | tf_op jit(solution)/shard_map/psum | solution.py:30
  35.0 312.1 %all-reduce.9.cloned.1.call-start = ((), (), s32[]{:S(2)}) async-start(), calls=%async_computation.1 | async-start | bytes 1769472 | tf_op jit(solution)/shard_map/psum | solution.py:68
  110.5 4.0 %copy-start.1 = (f32[96,256]{1,0:T(8,128)S(1)}, f32[96,256]{1,0:T(8,128)}, u32[]{:S(2)}) copy-start(f32[96,256]{1,0:T(8,128)} %custom-call.1) | copy-start | bytes 294916
  110.5 4.0 %copy-start.3 = (f32[96,8,256]{2,1,0:T(8,128)S(1)}, f32[96,8,256]{2,1,0:T(8,128)}, u32[]{:S(2)}) copy-start(f32[96,8,256]{2,1,0:T(8,128)} %custom-call) | copy-start | bytes 2359300
  217.9 0.6 copy-start.2
  218.0 0.9 copy-start.4
Sparse Core Ops, SparseCore 0:
  35.1 55.8 all-reduce.6
  219.0 128.0 all-reduce.8
where the time goes:
time: 362 us; the launch traced here: 357 us
  waiting for transfers between devices  166 us (46%)
  matrix products  66.6 us (18%)
  other arithmetic  42.5 us (12%)
  blocking collectives  34.1 us (9%)
  local copies, waits for them, and re-layouts  32.6 us (9%)
  between operations  14.8 us (4%)
    psum x1, waiting for transfers between devices, body(): lax.psum((code_sums.reshape(feature_width, CODEWORDS), code_counts), ('li...  127 us
    dot_general x12, matrix products, accumulate(): jnp.einsum('pmd,pmk->mdk', rot_blk, onehot, preferred_element_type=jnp.fl...  60.6 us
    psum x1, waiting for transfers between devices, body(): total_sum, total_mass = lax.psum((partial_sum, partial_mass), 'points')  39 us
    reduce_sum x12, other arithmetic, accumulate(): code_counts = code_counts + jnp.sum(onehot, axis=0, dtype=jnp.float32)  29.6 us
    psum x1, blocking collectives, body(): total_sum, total_mass = lax.psum((partial_sum, partial_mass), 'points')  13.8 us
    dynamic_slice x12, local copies, waits for them, and re-layouts, body(): lax.scan(accumulate, initial, (rotated.reshape(block_count, block_rows, s...  12.4 us
    unnamed x1, blocking collectives  11.3 us
    all_gather x1, blocking collectives, body(): lax.all_gather(weighted, 'lists', axis=0, tiled=True)  9.01 us
  transfers between devices with their start and end apart: 2, of which 2 were waited for; matrix products, arithmetic and copies ran while one was open for 1% of the time, Pallas kernels for 0%

commit v1 on v0

--- a/solution.py
+++ b/solution.py
@@ -66,7 +66,7 @@
         ),
     )
     total_sums, total_counts = lax.psum(
-        (code_sums.reshape(feature_width, CODEWORDS), code_counts), ("lists", "points")
+        lax.psum((code_sums.reshape(feature_width, CODEWORDS), code_counts), "points"), "lists"
     )
     means = total_sums.reshape(subspaces, sub_width, CODEWORDS) / (1.0 + total_counts[:, None, :])
     return (merged, means.reshape(feature_width, CODEWORDS))

time: 362 us -> 344 us (0.950)
  waiting for transfers between devices: 166 us -> 147 us
    psum x1 -> x2, waiting for transfers between devices: 127 us -> 108 us  [the longest x1 56.4 us: body(): lax.psum((code_sums.reshape(feature_width, CODEWORDS), code_counts), 'poi...]
  transfers between devices with their start and end apart: 2 -> 3, of which waited for: 2 -> 3; matrix products, arithmetic and copies ran while one was open for 1% -> 1% of each run, Pallas kernels for 0% -> 0%
where the time goes in v1:
time: 344 us; the launch traced here: 338 us
  waiting for transfers between devices  147 us (43%)
  matrix products  66.7 us (19%)
  other arithmetic  42.5 us (12%)
  blocking collectives  34.1 us (10%)
  local copies, waits for them, and re-layouts  32.6 us (9%)
  between operations  14.5 us (4%)
    dot_general x12, matrix products, accumulate(): jnp.einsum('pmd,pmk->mdk', rot_blk, onehot, preferred_element_type=jnp.fl...  60.6 us
    psum x1, waiting for transfers between devices, body(): lax.psum((code_sums.reshape(feature_width, CODEWORDS), code_counts), 'poi...  56.4 us
    psum x1, waiting for transfers between devices, body(): lax.psum(lax.psum((code_sums.reshape(feature_width, CODEWORDS), code_coun...  52 us
    psum x1, waiting for transfers between devices, body(): total_sum, total_mass = lax.psum((partial_sum, partial_mass), 'points')  39 us
    reduce_sum x12, other arithmetic, accumulate(): code_counts = code_counts + jnp.sum(onehot, axis=0, dtype=jnp.float32)  29.6 us
    psum x1, blocking collectives, body(): total_sum, total_mass = lax.psum((partial_sum, partial_mass), 'points')  13.8 us
    dynamic_slice x12, local copies, waits for them, and re-layouts, body(): lax.scan(accumulate, initial, (rotated.reshape(block_count, block_rows, s...  12.4 us
    unnamed x1, blocking collectives  11.3 us
  transfers between devices with their start and end apart: 3, of which 3 were waited for; matrix products, arithmetic and copies ran while one was open for 1% of the time, Pallas kernels for 0%

profile of v1, /device:TPU:0, one launch (start us, length us, event | category | flops | bytes accessed | tf_op | source)
XLA Modules:
  0.0 338.4 jit_solution(5957835746227253526)
XLA Ops:
  11.5 11.3 %all-reduce.3 = (f32[128]{0:T(128)S(1)}, f32[128]{0:T(128)S(1)}) all-reduce(f32[128]{0:T(128)S(1)} %convert_dynamic-update-slice_fusion, f32[128]{0:T(128)S(1)} %convert_dynamic-update-slice_fusion.1), channel_id=1, replica_groups=mesh['lists'=4,'points'=8] {'lists'}, use_global_device_ids=true, to_apply=%add | all-reduce | flops 256 | bytes 2048
  23.8 9.0 %all_gather.10 = f32[128,768]{1,0:T(8,128)S(1)} all-gather(f32[32,768]{1,0:T(8,128)S(1)} %broadcast_multiply_fusion), channel_id=1, replica_groups=mesh['lists'=4,'points'=8] {'lists'}, dimensions={0}, use_global_device_ids=true | all-gather | bytes 491520 | tf_op jit(solution)/shard_map/all_gather | solution.py:17
  36.5 13.8 %psum.43 = f32[128]{0:T(128)S(1)} all-reduce(f32[128]{0:T(128)S(1)} %scatter_custom_fusion.1), channel_id=1, replica_groups=mesh['lists'=4,'points'=8] {'points'}, use_global_device_ids=true, to_apply=%region_3.4 | all-reduce | flops 128 | bytes 1024 | tf_op jit(solution)/shard_map/psum | solution.py:30
  52.1 39.0 %all-reduce.9.cloned.1.call-done = f32[128,768]{1,0:T(8,128)} async-done(((f32[128,768]{1,0:T(8,128)}), f32[128,768]{1,0:T(8,128)}) %all-reduce.9.cloned.1.call-update) | async-done | bytes 393232 | tf_op jit(solution)/shard_map/psum | solution.py:30
  92.9 5.7 %gather_fusion = bf16[1536,768]{1,0:T(8,128)(2,1)} fusion(bf16[128,768]{1,0:T(8,128)(2,1)S(1)} %get-tuple-element.83, s32[2048]{0:T(1024)S(1)} %pad_clamp_fusion), kind=kCustom, calls=%fused_computation | custom fusion | bytes 4724736 | tf_op jit(solution)/shard_map/jit(_take)/gather | solution.py:36
  98.6 6.0 %convolution_convert_fusion = bf16[1536,768]{1,0:T(8,128)(2,1)} fusion(bf16[768,768]{1,0:T(8,128)(2,1)S(1)} %copy-done, bf16[1536,768]{1,0:T(8,128)(2,1)} %param.12, bf16[1536,768]{1,0:T(8,128)(2,1)} %gather_fusion, pred[1536]{0:T(1024)(128)(4,1)S(1)} %compare_and_fusion), kind=kOutput, calls=%fused_computation.16 | convolution fusion | flops 1819017216 | bytes 8259072 | tf_op jit(solution)/shard_map/dot_general | solution.py:38
  104.6 2.8 copy.10
  107.5 3.1 reshape.29
  110.5 4.0 %copy.11 = bf16[12,128,96,8]{1,3,2,0:T(8,128)(2,1)} copy(bf16[12,128,96,8]{1,0,3,2:T(8,128)(2,1)} %reshape.29) | data formatting | bytes 4718592
  114.5 103.4 %while.13 = (s32[]{:T(128)}, f32[96,8,256]{2,1,0:T(8,128)S(1)}, f32[96,256]{1,0:T(8,128)S(1)}, bf16[12,128,96,8]{1,3,2,0:T(8,128)(2,1)}, s32[12,128,96]{1,0,2:T(8,128)}, /*index=5*/s32[]{:T(128)}, s32[]{:T(128)}) while((s32[]{:T(128)}, f32[96,8,256]{2,1,0:T(8,128)S(1)}, f32[96,256]{1,0:T(8,128)S(1)}, ...), condition=%wide.region_6.7_spmd.clone, body=%wide.region_4.6_spmd.clone.sunk | while | flops 66478080 | bytes 2359900 | solution.py:60
  115.6 5.1 %fusion.23 = f32[96,8,256]{2,1,0:T(8,128)S(1)} fusion(s32[128,96]{0,1:T(8,128)S(1)} %bitcast.19, f32[96,8,256]{2,1,0:T(8,128)S(1)} %get-tuple-element.126, pred[]{:T(512)S(6)} %compare.3, bf16[12,128,96,8]{1,3,2,0:T(8,128)(2,1)} %get-tuple-element.135, s32[]{:T(128)} %get-tuple-element.125), kind=kOutput, calls=%fused_computation.9.clone.1 | convolution fusion | flops 53870592 | bytes 1819137 | tf_op jit(solution)/shard_map/while/body/eval_jaxpr/pmd,pmk->mdk/dot_general | solution.py:50
  120.6 2.5 convert_reduce_fusion.2
  124.2 5.1 %fusion.23 = f32[96,8,256]{2,1,0:T(8,128)S(1)} fusion(s32[128,96]{0,1:T(8,128)S(1)} %bitcast.19, f32[96,8,256]{2,1,0:T(8,128)S(1)} %get-tuple-element.126, pred[]{:T(512)S(6)} %compare.3, bf16[12,128,96,8]{1,3,2,0:T(8,128)(2,1)} %get-tuple-element.135, s32[]{:T(128)} %get-tuple-element.125), kind=kOutput, calls=%fused_computation.9.clone.1 | convolution fusion | flops 53870592 | bytes 1819137 | tf_op jit(solution)/shard_map/while/body/eval_jaxpr/pmd,pmk->mdk/dot_general | solution.py:50
  129.3 2.5 convert_reduce_fusion.2
  132.8 5.1 %fusion.23 = f32[96,8,256]{2,1,0:T(8,128)S(1)} fusion(s32[128,96]{0,1:T(8,128)S(1)} %bitcast.19, f32[96,8,256]{2,1,0:T(8,128)S(1)} %get-tuple-element.126, pred[]{:T(512)S(6)} %compare.3, bf16[12,128,96,8]{1,3,2,0:T(8,128)(2,1)} %get-tuple-element.135, s32[]{:T(128)} %get-tuple-element.125), kind=kOutput, calls=%fused_computation.9.clone.1 | convolution fusion | flops 53870592 | bytes 1819137 | tf_op jit(solution)/shard_map/while/body/eval_jaxpr/pmd,pmk->mdk/dot_general | solution.py:50
  137.9 2.5 convert_reduce_fusion.2
  141.4 5.1 %fusion.23 = f32[96,8,256]{2,1,0:T(8,128)S(1)} fusion(s32[128,96]{0,1:T(8,128)S(1)} %bitcast.19, f32[96,8,256]{2,1,0:T(8,128)S(1)} %get-tuple-element.126, pred[]{:T(512)S(6)} %compare.3, bf16[12,128,96,8]{1,3,2,0:T(8,128)(2,1)} %get-tuple-element.135, s32[]{:T(128)} %get-tuple-element.125), kind=kOutput, calls=%fused_computation.9.clone.1 | convolution fusion | flops 53870592 | bytes 1819137 | tf_op jit(solution)/shard_map/while/body/eval_jaxpr/pmd,pmk->mdk/dot_general | solution.py:50
  146.5 2.5 convert_reduce_fusion.2
  150.1 5.1 %fusion.23 = f32[96,8,256]{2,1,0:T(8,128)S(1)} fusion(s32[128,96]{0,1:T(8,128)S(1)} %bitcast.19, f32[96,8,256]{2,1,0:T(8,128)S(1)} %get-tuple-element.126, pred[]{:T(512)S(6)} %compare.3, bf16[12,128,96,8]{1,3,2,0:T(8,128)(2,1)} %get-tuple-element.135, s32[]{:T(128)} %get-tuple-element.125), kind=kOutput, calls=%fused_computation.9.clone.1 | convolution fusion | flops 53870592 | bytes 1819137 | tf_op jit(solution)/shard_map/while/body/eval_jaxpr/pmd,pmk->mdk/dot_general | solution.py:50
  155.1 2.5 convert_reduce_fusion.2
  158.7 5.1 %fusion.23 = f32[96,8,256]{2,1,0:T(8,128)S(1)} fusion(s32[128,96]{0,1:T(8,128)S(1)} %bitcast.19, f32[96,8,256]{2,1,0:T(8,128)S(1)} %get-tuple-element.126, pred[]{:T(512)S(6)} %compare.3, bf16[12,128,96,8]{1,3,2,0:T(8,128)(2,1)} %get-tuple-element.135, s32[]{:T(128)} %get-tuple-element.125), kind=kOutput, calls=%fused_computation.9.clone.1 | convolution fusion | flops 53870592 | bytes 1819137 | tf_op jit(solution)/shard_map/while/body/eval_jaxpr/pmd,pmk->mdk/dot_general | solution.py:50
  167.3 5.1 %fusion.23 = f32[96,8,256]{2,1,0:T(8,128)S(1)} fusion(s32[128,96]{0,1:T(8,128)S(1)} %bitcast.19, f32[96,8,256]{2,1,0:T(8,128)S(1)} %get-tuple-element.126, pred[]{:T(512)S(6)} %compare.3, bf16[12,128,96,8]{1,3,2,0:T(8,128)(2,1)} %get-tuple-element.135, s32[]{:T(128)} %get-tuple-element.125), kind=kOutput, calls=%fused_computation.9.clone.1 | convolution fusion | flops 53870592 | bytes 1819137 | tf_op jit(solution)/shard_map/while/body/eval_jaxpr/pmd,pmk->mdk/dot_general | solution.py:50
  172.3 2.5 convert_reduce_fusion.2
  175.9 5.1 %fusion.23 = f32[96,8,256]{2,1,0:T(8,128)S(1)} fusion(s32[128,96]{0,1:T(8,128)S(1)} %bitcast.19, f32[96,8,256]{2,1,0:T(8,128)S(1)} %get-tuple-element.126, pred[]{:T(512)S(6)} %compare.3, bf16[12,128,96,8]{1,3,2,0:T(8,128)(2,1)} %get-tuple-element.135, s32[]{:T(128)} %get-tuple-element.125), kind=kOutput, calls=%fused_computation.9.clone.1 | convolution fusion | flops 53870592 | bytes 1819137 | tf_op jit(solution)/shard_map/while/body/eval_jaxpr/pmd,pmk->mdk/dot_general | solution.py:50
  181.0 2.5 convert_reduce_fusion.2
  184.5 5.1 %fusion.23 = f32[96,8,256]{2,1,0:T(8,128)S(1)} fusion(s32[128,96]{0,1:T(8,128)S(1)} %bitcast.19, f32[96,8,256]{2,1,0:T(8,128)S(1)} %get-tuple-element.126, pred[]{:T(512)S(6)} %compare.3, bf16[12,128,96,8]{1,3,2,0:T(8,128)(2,1)} %get-tuple-element.135, s32[]{:T(128)} %get-tuple-element.125), kind=kOutput, calls=%fused_computation.9.clone.1 | convolution fusion | flops 53870592 | bytes 1819137 | tf_op jit(solution)/shard_map/while/body/eval_jaxpr/pmd,pmk->mdk/dot_general | solution.py:50
  193.1 5.1 %fusion.23 = f32[96,8,256]{2,1,0:T(8,128)S(1)} fusion(s32[128,96]{0,1:T(8,128)S(1)} %bitcast.19, f32[96,8,256]{2,1,0:T(8,128)S(1)} %get-tuple-element.126, pred[]{:T(512)S(6)} %compare.3, bf16[12,128,96,8]{1,3,2,0:T(8,128)(2,1)} %get-tuple-element.135, s32[]{:T(128)} %get-tuple-element.125), kind=kOutput, calls=%fused_computation.9.clone.1 | convolution fusion | flops 53870592 | bytes 1819137 | tf_op jit(solution)/shard_map/while/body/eval_jaxpr/pmd,pmk->mdk/dot_general | solution.py:50
  201.8 5.1 %fusion.23 = f32[96,8,256]{2,1,0:T(8,128)S(1)} fusion(s32[128,96]{0,1:T(8,128)S(1)} %bitcast.19, f32[96,8,256]{2,1,0:T(8,128)S(1)} %get-tuple-element.126, pred[]{:T(512)S(6)} %compare.3, bf16[12,128,96,8]{1,3,2,0:T(8,128)(2,1)} %get-tuple-element.135, s32[]{:T(128)} %get-tuple-element.125), kind=kOutput, calls=%fused_computation.9.clone.1 | convolution fusion | flops 53870592 | bytes 1819137 | tf_op jit(solution)/shard_map/while/body/eval_jaxpr/pmd,pmk->mdk/dot_general | solution.py:50
  210.4 5.1 %fusion.23 = f32[96,8,256]{2,1,0:T(8,128)S(1)} fusion(s32[128,96]{0,1:T(8,128)S(1)} %bitcast.19, f32[96,8,256]{2,1,0:T(8,128)S(1)} %get-tuple-element.126, pred[]{:T(512)S(6)} %compare.3, bf16[12,128,96,8]{1,3,2,0:T(8,128)(2,1)} %get-tuple-element.135, s32[]{:T(128)} %get-tuple-element.125), kind=kOutput, calls=%fused_computation.9.clone.1 | convolution fusion | flops 53870592 | bytes 1819137 | tf_op jit(solution)/shard_map/while/body/eval_jaxpr/pmd,pmk->mdk/dot_general | solution.py:50
  215.4 2.5 convert_reduce_fusion.2
  218.9 56.4 %all-reduce.11.cloned.1.call-done = (f32[768,256]{1,0:T(8,128)}, f32[96,256]{1,0:T(8,128)}) async-done(((f32[768,256]{1,0:T(8,128)}, f32[96,256]{1,0:T(8,128)}), (f32[768,256]{1,0:T(8,128)}, f32[96,256]{1,0:T(8,128)})) %all-reduce.11.cloned.1.call-update) | async-done | bytes 884752 | tf_op jit(solution)/shard_map/psum | solution.py:69
  276.8 52.0 %all-reduce.13.cloned.1.call-done = (f32[768,256]{1,0:T(8,128)}, f32[96,256]{1,0:T(8,128)}) async-done(((f32[768,256]{1,0:T(8,128)}, f32[96,256]{1,0:T(8,128)}), (f32[768,256]{1,0:T(8,128)}, f32[96,256]{1,0:T(8,128)})) %all-reduce.13.cloned.1.call-update) | async-done | bytes 884752 | tf_op jit(solution)/shard_map/psum | solution.py:68
  (69 shorter events, 40.0 us)
Async XLA Ops:
  7.2 91.4 %copy-start = (bf16[768,768]{1,0:T(8,128)(2,1)S(1)}, bf16[768,768]{1,0:T(8,128)(2,1)}, u32[]{:S(2)}) copy-start(bf16[768,768]{1,0:T(8,128)(2,1)} %param.15) | copy-start | bytes 3538948
  7.2 44.9 %copy-start.6 = (s32[1536]{0:T(1024)S(1)}, s32[1536]{0:T(1024)}, u32[]{:S(2)}) copy-start(s32[1536]{0:T(1024)} %param.13) | copy-start | bytes 18436
  7.2 43.8 %copy-start.5 = (s32[1536,96]{0,1:T(8,128)S(1)}, s32[1536,96]{0,1:T(8,128)}, u32[]{:S(2)}) copy-start(s32[1536,96]{0,1:T(8,128)} %param.14) | copy-start | bytes 1769476
  7.2 83.8 %all-reduce.9.cloned.1.call-start = ((), (), s32[]{:S(2)}) async-start(), calls=%async_computation | async-start | bytes 786432 | tf_op jit(solution)/shard_map/psum | solution.py:30
  35.0 240.4 %all-reduce.11.cloned.1.call-start = ((), (), s32[]{:S(2)}) async-start(), calls=%async_computation.1 | async-start | bytes 1769472 | tf_op jit(solution)/shard_map/psum | solution.py:69
  110.5 4.0 %copy-start.1 = (f32[96,256]{1,0:T(8,128)S(1)}, f32[96,256]{1,0:T(8,128)}, u32[]{:S(2)}) copy-start(f32[96,256]{1,0:T(8,128)} %custom-call.1) | copy-start | bytes 294916
  110.5 4.0 %copy-start.3 = (f32[96,8,256]{2,1,0:T(8,128)S(1)}, f32[96,8,256]{2,1,0:T(8,128)}, u32[]{:S(2)}) copy-start(f32[96,8,256]{2,1,0:T(8,128)} %custom-call) | copy-start | bytes 2359300
  218.0 0.6 copy-start.2
  218.0 0.9 copy-start.4
  218.9 110.0 %all-reduce.13.cloned.1.call-start = ((), (), s32[]{:S(2)}) async-start(), calls=%async_computation.2 | async-start | bytes 1769472 | tf_op jit(solution)/shard_map/psum | solution.py:68
Sparse Core Ops, SparseCore 0:
  35.2 55.8 all-reduce.8
  219.0 56.3 all-reduce.10
  278.5 50.2 all-reduce.12
